TPU v7x, 256 devices: a whole 4x4x8 slice. The times are simulated.
256 devices in a mesh: row: 16 (over z, y_lo), col: 16 (over y_hi, x, core).
Axes of the slice: x: 4, y: 4 (y_hi: 2, y_lo: 2; y = y_hi * 2 + y_lo), z: 8, core: 2. Of those that a mesh axis runs over, the one named last changes fastest.
Arguments:
- core_blocks: float32 [64, 2048, 128], P('row', 'col'), may hold values from -6 to 6
- block_coords: int32 [64, 32], replicated, may hold values from 0 to 9, as said below
- band_vectors: float32 [16, 16, 128], P('col'), may hold values from -6 to 6
- band_blocks: int32 [16, 16], P('col'), may hold values from 0 to 159, as said below
- spread: float32 [], replicated, may hold values from 12 to 24
Outputs:
- purified: float32 [64, 2048, 128], P('row', 'col')
Inputs may be any that keep to these rules, and one draw needn't show every extreme that they name: `block_coords`: the first entry of a slot is a local block row below 10, the second a local block column below 10; the 4 slots of one tile name distinct blocks. `band_blocks`: the 16 block rows of one band are distinct.
All inputs are finite; a program needn't handle non-finite values.
Results may differ from a plain program's by a relative error of at most 0.0003.
Values sent between devices are 32-bit elements; how exact they have to be, the bound alone decides.
A program may use at most 64 MiB of HBM per device.

v0:
```python
import jax
import jax.numpy as jnp
from jax import lax
from jax.sharding import PartitionSpec as P

NB = 160
highest = lax.Precision.HIGHEST


def shifted(block, axis, distance):
    devices = range(lax.axis_size(axis))
    route = [((i - distance) % len(devices), i) for i in devices]
    return lax.ppermute(block, axis, route)


def exchange_term(vectors, blocks, block_rows, block_cols):
    hit_row = (blocks[:, :, None] == block_rows[None, None, :]).astype(jnp.float32)
    hit_col = (blocks[:, :, None] == block_cols[None, None, :]).astype(jnp.float32)
    vec_row = jnp.einsum("bln,blx->bnx", hit_row, vectors, precision=highest)
    vec_col = jnp.einsum("bln,blx->bnx", hit_col, vectors, precision=highest)
    return -jnp.einsum("bnx,bny->nxy", vec_row, vec_col, precision=highest)


def tile_layout(layout, tile_row, tile_col):
    slots = layout.shape[1]
    start = (tile_row, jnp.int32(0), tile_col, jnp.int32(0))
    return lax.dynamic_slice(layout, start, (1, slots, 1, 2)).reshape(slots, 2)


def link_weights(targets, left_local, piece, right_local, tile_rows):
    row_target = targets[:, None, None, 0]
    col_target = targets[:, None, None, 1]
    row_left = left_local[None, :, None, 0]
    col_left = left_local[None, :, None, 1]
    row_right = right_local[None, None, :, 0]
    col_right = right_local[None, None, :, 1]
    keep = (row_left == row_target) & (col_left // tile_rows == piece)
    keep = keep & (col_left % tile_rows == row_right) & (col_right == col_target)
    return keep.astype(jnp.float32)


def accumulate(
    total, targets, left_blocks, left_local, piece, right_blocks, right_local, tile_rows
):
    weight = link_weights(targets, left_local, piece, right_local, tile_rows)
    pairs = jnp.einsum("axk,bky->axby", left_blocks, right_blocks, precision=highest)
    return total + jnp.einsum("tab,axby->txy", weight, pairs, precision=highest)


def advance(window):
    moved = shifted(window[0], "col", -1)
    return jnp.concatenate([window[1:], moved[None]], axis=0)


def align_right(right, this_col, ratio):
    row_count = lax.axis_size("row")
    amount = ratio * this_col % row_count
    for place in range((row_count - 1).bit_length()):
        moved = shifted(right, "row", -(1 << place))
        right = jnp.where(amount >> place & 1 == 1, moved, right)
    return right


def align_left(left, this_row, ratio):
    column_count = lax.axis_size("col")
    window = jnp.stack([left] * ratio)
    amount = this_row // ratio
    for place in range((column_count - 1).bit_length()):
        moved = shifted(window, "col", -(1 << place))
        window = jnp.where(amount >> place & 1 == 1, moved, window)
    return window


def shifted_product(left, right, layout, targets, this_row, this_col, tile_rows, ratio):
    row_count = lax.axis_size("row")
    window = align_left(left, this_row, ratio)

    def step_body(step, carry):
        total, window, right = carry
        source = (this_row + ratio * this_col + step) % row_count
        left_local = tile_layout(layout, this_row, source // ratio)
        right_local = tile_layout(layout, source, this_col)
        total = accumulate(
            total, targets, window[0], left_local, source % ratio, right, right_local, tile_rows
        )
        window = advance(window)
        right = shifted(right, "row", -1)
        return (total, window, right)

    total, window, right = lax.fori_loop(
        0, row_count, step_body, (jnp.zeros_like(left), window, right)
    )
    return (total, right)


def on_device(core_blocks, block_coords, band_vectors, band_blocks, spread):
    row_count = lax.axis_size("row")
    column_count = lax.axis_size("col")
    tile_rows = NB // row_count
    tile_columns = NB // column_count
    ratio = row_count // column_count
    slots = core_blocks.shape[0]
    this_row = lax.axis_index("row")
    this_col = lax.axis_index("col")
    layout = block_coords.reshape(row_count, slots, column_count, 2)
    targets = tile_layout(layout, this_row, this_col)
    vectors, blocks = (
        lax.all_gather(band_vectors, "col", axis=0, tiled=True),
        lax.all_gather(band_blocks, "col", axis=0, tiled=True),
    )
    block_rows = this_row * tile_rows + targets[:, 0]
    block_cols = this_col * tile_columns + targets[:, 1]
    exchange = exchange_term(vectors, blocks, block_rows, block_cols)
    fock = core_blocks + exchange
    scaled = fock / spread
    right = align_right(scaled, this_col, ratio)
    square, right = shifted_product(
        scaled, right, layout, targets, this_row, this_col, tile_rows, ratio
    )
    cube, right = shifted_product(
        square, right, layout, targets, this_row, this_col, tile_rows, ratio
    )
    return 1.5 * fock - 2.0 * spread * cube


def solution(mesh):
    placed = (P("row", "col", None), P(), P("col", None, None), P("col", None), P())
    return jax.shard_map(
        on_device, mesh=mesh, in_specs=placed, out_specs=P("row", "col", None), check_vma=False
    )
```

profile of v0, /device:TPU:6, one launch (start us, length us, event | category | flops | bytes accessed | tf_op | source)
XLA Modules:
  0.0 540.6 jit_solution(16270872847556958908)
XLA Ops:
  1.4 18.7 %all_gather.7 = f32[16,16,128]{2,1,0:T(8,128)S(1)} all-gather(f32[1,16,128]{2,1,0:T(8,128)S(1)} %copy-done.1), channel_id=1, replica_groups=mesh['row'=16,'col'=16] {'col'}, dimensions={0}, use_global_device_ids=true | all-gather | bytes 139264 | tf_op jit(solution)/shard_map/all_gather | solution.py:108
  20.8 21.4 %all-gather = s32[16,1,16]{2,1,0:T(1,128)S(1)} all-gather(s32[1,1,16]{2,1,0:T(1,128)S(1)} %bitcast.174), channel_id=1, replica_groups=mesh['row'=16,'col'=16] {'col'}, dimensions={0}, use_global_device_ids=true | all-gather | bytes 1088 | tf_op jit(solution)/shard_map/all_gather | solution.py:109
  44.1 6.9 %collective-permute-start.8 = (f32[4,128,128]{2,1,0:T(8,128)S(1)}, f32[4,128,128]{2,1,0:T(8,128)S(1)}, u32[]{:S(2)}, u32[]{:S(2)}) collective-permute-start(f32[4,128,128]{2,1,0:T(8,128)S(1)} %get-tuple-element.699), channel_id=1, source_target_pairs={{16,0},{32,16},{48,32},{64,48},{80,64},{96,80},{112,96},{128,112},... | collective-permute-start | bytes 786440 | tf_op jit(solution)/shard_map/ppermute | solution.py:13
  51.0 6.1 %collective-permute-done.8 = f32[4,128,128]{2,1,0:T(8,128)S(1)} collective-permute-done((f32[4,128,128]{2,1,0:T(8,128)S(1)}, f32[4,128,128]{2,1,0:T(8,128)S(1)}, u32[]{:S(2)}, u32[]{:S(2)}) %collective-permute-start.8) | collective-permute-done | bytes 262176 | tf_op jit(solution)/shard_map/ppermute | solution.py:13
  72.6 5.4 collective-permute-done.10
  86.7 5.6 %collective-permute-done.11 = f32[4,128,128]{2,1,0:T(8,128)S(1)} collective-permute-done((f32[4,128,128]{2,1,0:T(8,128)S(1)}, f32[4,128,128]{2,1,0:T(8,128)S(1)}, u32[]{:S(2)}, u32[]{:S(2)}) %collective-permute-start.11) | collective-permute-done | bytes 262176 | tf_op jit(solution)/shard_map/ppermute | solution.py:13
  92.3 208.9 %while.42 = (s32[]{:T(128)}, f32[4,128,128]{2,0,1:T(4,128)S(1)}, f32[1,4,128,128]{3,2,1,0:T(8,128)S(1)}, f32[4,128,128]{2,1,0:T(8,128)S(1)}, s32[]{:T(128)}, /*i...) while((s32[]{:T(128)}, f32[4,128,128]{2,0,1:T(4,128)S(1)}, ...), condition=%wide.region_1.2_spmd.clone, body=%wide.region_0.1_spmd.clone.sunk | while | flops 415367424 | bytes 6292374 | solution.py:90
  92.5 8.7 %collective-permute-start.1 = (f32[4,128,128]{2,1,0:T(8,128)S(1)}, f32[4,128,128]{2,1,0:T(8,128)S(1)}, u32[]{:S(2)}, u32[]{:S(2)}) collective-permute-start(f32[4,128,128]{2,1,0:T(8,128)S(1)} %copy.54), channel_id=1, source_target_pairs={{16,0},{32,16},{48,32},{64,48},{80,64},{96,80},{112,96},{128,112},... | collective-permute-start | bytes 786440 | tf_op jit(solution)/shard_map/while/body/eval_jaxpr/ppermute | solution.py:13
  109.1 6.0 %collective-permute-start.1 = (f32[4,128,128]{2,1,0:T(8,128)S(1)}, f32[4,128,128]{2,1,0:T(8,128)S(1)}, u32[]{:S(2)}, u32[]{:S(2)}) collective-permute-start(f32[4,128,128]{2,1,0:T(8,128)S(1)} %copy.54), channel_id=1, source_target_pairs={{16,0},{32,16},{48,32},{64,48},{80,64},{96,80},{112,96},{128,112},... | collective-permute-start | bytes 786440 | tf_op jit(solution)/shard_map/while/body/eval_jaxpr/ppermute | solution.py:13
  118.1 5.9 %collective-permute-done.1 = f32[4,128,128]{2,1,0:T(8,128)S(1)} collective-permute-done((f32[4,128,128]{2,1,0:T(8,128)S(1)}, f32[4,128,128]{2,1,0:T(8,128)S(1)}, u32[]{:S(2)}, u32[]{:S(2)}) %collective-permute-start.1) | collective-permute-done | bytes 262176 | tf_op jit(solution)/shard_map/while/body/eval_jaxpr/ppermute | solution.py:13
  169.1 5.9 %collective-permute-done.1 = f32[4,128,128]{2,1,0:T(8,128)S(1)} collective-permute-done((f32[4,128,128]{2,1,0:T(8,128)S(1)}, f32[4,128,128]{2,1,0:T(8,128)S(1)}, u32[]{:S(2)}, u32[]{:S(2)}) %collective-permute-start.1) | collective-permute-done | bytes 262176 | tf_op jit(solution)/shard_map/while/body/eval_jaxpr/ppermute | solution.py:13
  220.0 5.9 %collective-permute-done.1 = f32[4,128,128]{2,1,0:T(8,128)S(1)} collective-permute-done((f32[4,128,128]{2,1,0:T(8,128)S(1)}, f32[4,128,128]{2,1,0:T(8,128)S(1)}, u32[]{:S(2)}, u32[]{:S(2)}) %collective-permute-start.1) | collective-permute-done | bytes 262176 | tf_op jit(solution)/shard_map/while/body/eval_jaxpr/ppermute | solution.py:13
  270.9 5.9 %collective-permute-done.1 = f32[4,128,128]{2,1,0:T(8,128)S(1)} collective-permute-done((f32[4,128,128]{2,1,0:T(8,128)S(1)}, f32[4,128,128]{2,1,0:T(8,128)S(1)}, u32[]{:S(2)}, u32[]{:S(2)}) %collective-permute-start.1) | collective-permute-done | bytes 262176 | tf_op jit(solution)/shard_map/while/body/eval_jaxpr/ppermute | solution.py:13
  305.5 10.0 %collective-permute-done.13 = f32[1,4,128,128]{3,2,1,0:T(8,128)S(1)} collective-permute-done((f32[1,4,128,128]{3,2,1,0:T(8,128)S(1)}, f32[1,4,128,128]{3,2,1,0:T(8,128)S(1)}, u32[]{:S(2)}, u32[]{:S(2)}) %collective-permute-start.13) | collective-permute-done | bytes 262176 | tf_op jit(solution)/shard_map/ppermute | solution.py:13
  315.8 10.1 %collective-permute-done.14 = f32[1,4,128,128]{3,2,1,0:T(8,128)S(1)} collective-permute-done((f32[1,4,128,128]{3,2,1,0:T(8,128)S(1)}, f32[1,4,128,128]{3,2,1,0:T(8,128)S(1)}, u32[]{:S(2)}, u32[]{:S(2)}) %collective-permute-start.14) | collective-permute-done | bytes 262176 | tf_op jit(solution)/shard_map/ppermute | solution.py:13
  328.9 5.9 %collective-permute-done.15 = f32[1,4,128,128]{3,2,1,0:T(8,128)S(1)} collective-permute-done((f32[1,4,128,128]{3,2,1,0:T(8,128)S(1)}, f32[1,4,128,128]{3,2,1,0:T(8,128)S(1)}, u32[]{:S(2)}, u32[]{:S(2)}) %collective-permute-start.15) | collective-permute-done | bytes 262176 | tf_op jit(solution)/shard_map/ppermute | solution.py:13
  334.8 205.0 %while.43 = (s32[]{:T(128)}, f32[4,128,128]{2,0,1:T(4,128)S(1)}, f32[1,4,128,128]{3,2,1,0:T(8,128)S(1)}, f32[4,128,128]{2,1,0:T(8,128)S(1)}, s32[]{:T(128)}, /*i...) while((s32[]{:T(128)}, f32[4,128,128]{2,0,1:T(4,128)S(1)}, ...), condition=%wide.region_3.4_spmd.clone, body=%wide.region_2.3_spmd.clone.sunk | while | flops 415367424 | bytes 6292374 | solution.py:90
  342.8 5.5 %collective-permute-done.3 = f32[4,128,128]{2,1,0:T(8,128)S(1)} collective-permute-done((f32[4,128,128]{2,1,0:T(8,128)S(1)}, f32[4,128,128]{2,1,0:T(8,128)S(1)}, u32[]{:S(2)}, u32[]{:S(2)}) %collective-permute-start.3) | collective-permute-done | bytes 262176 | tf_op jit(solution)/shard_map/while/body/eval_jaxpr/ppermute | solution.py:13
  395.0 5.7 %collective-permute-done.3 = f32[4,128,128]{2,1,0:T(8,128)S(1)} collective-permute-done((f32[4,128,128]{2,1,0:T(8,128)S(1)}, f32[4,128,128]{2,1,0:T(8,128)S(1)}, u32[]{:S(2)}, u32[]{:S(2)}) %collective-permute-start.3) | collective-permute-done | bytes 262176 | tf_op jit(solution)/shard_map/while/body/eval_jaxpr/ppermute | solution.py:13
  432.8 5.2 collective-permute-done.3
  446.0 5.7 %collective-permute-done.3 = f32[4,128,128]{2,1,0:T(8,128)S(1)} collective-permute-done((f32[4,128,128]{2,1,0:T(8,128)S(1)}, f32[4,128,128]{2,1,0:T(8,128)S(1)}, u32[]{:S(2)}, u32[]{:S(2)}) %collective-permute-start.3) | collective-permute-done | bytes 262176 | tf_op jit(solution)/shard_map/while/body/eval_jaxpr/ppermute | solution.py:13
  483.8 5.2 collective-permute-done.3
  496.9 5.7 %collective-permute-done.3 = f32[4,128,128]{2,1,0:T(8,128)S(1)} collective-permute-done((f32[4,128,128]{2,1,0:T(8,128)S(1)}, f32[4,128,128]{2,1,0:T(8,128)S(1)}, u32[]{:S(2)}, u32[]{:S(2)}) %collective-permute-start.3) | collective-permute-done | bytes 262176 | tf_op jit(solution)/shard_map/while/body/eval_jaxpr/ppermute | solution.py:13
  534.7 5.2 collective-permute-done.3
  (547 shorter events, 370.9 us)
Async XLA Ops:
  44.1 13.0 %collective-permute-start.8 = (f32[4,128,128]{2,1,0:T(8,128)S(1)}, f32[4,128,128]{2,1,0:T(8,128)S(1)}, u32[]{:S(2)}, u32[]{:S(2)}) collective-permute-start(f32[4,128,128]{2,1,0:T(8,128)S(1)} %get-tuple-element.699), channel_id=1, source_target_pairs={{16,0},{32,16},{48,32},{64,48},{80,64},{96,80},{112,96},{128,112},... | collective-permute-start | bytes 786440 | tf_op jit(solution)/shard_map/ppermute | solution.py:13
  78.0 14.3 %collective-permute-start.11 = (f32[4,128,128]{2,1,0:T(8,128)S(1)}, f32[4,128,128]{2,1,0:T(8,128)S(1)}, u32[]{:S(2)}, u32[]{:S(2)}) collective-permute-start(f32[4,128,128]{2,1,0:T(8,128)S(1)} %broadcast_select_fusion.2), channel_id=1, source_target_pairs={{128,0},{144,16},{160,32},{176,48},{192,64},{208,80},{224,96},{240... | collective-permute-start | bytes 786440 | tf_op jit(solution)/shard_map/ppermute | solution.py:13
  92.5 16.4 %collective-permute-start.1 = (f32[4,128,128]{2,1,0:T(8,128)S(1)}, f32[4,128,128]{2,1,0:T(8,128)S(1)}, u32[]{:S(2)}, u32[]{:S(2)}) collective-permute-start(f32[4,128,128]{2,1,0:T(8,128)S(1)} %copy.54), channel_id=1, source_target_pairs={{16,0},{32,16},{48,32},{64,48},{80,64},{96,80},{112,96},{128,112},... | collective-permute-start | bytes 786440 | tf_op jit(solution)/shard_map/while/body/eval_jaxpr/ppermute | solution.py:13
  109.1 15.0 %collective-permute-start.1 = (f32[4,128,128]{2,1,0:T(8,128)S(1)}, f32[4,128,128]{2,1,0:T(8,128)S(1)}, u32[]{:S(2)}, u32[]{:S(2)}) collective-permute-start(f32[4,128,128]{2,1,0:T(8,128)S(1)} %copy.54), channel_id=1, source_target_pairs={{16,0},{32,16},{48,32},{64,48},{80,64},{96,80},{112,96},{128,112},... | collective-permute-start | bytes 786440 | tf_op jit(solution)/shard_map/while/body/eval_jaxpr/ppermute | solution.py:13
  124.2 12.8 %collective-permute-start.1 = (f32[4,128,128]{2,1,0:T(8,128)S(1)}, f32[4,128,128]{2,1,0:T(8,128)S(1)}, u32[]{:S(2)}, u32[]{:S(2)}) collective-permute-start(f32[4,128,128]{2,1,0:T(8,128)S(1)} %copy.54), channel_id=1, source_target_pairs={{16,0},{32,16},{48,32},{64,48},{80,64},{96,80},{112,96},{128,112},... | collective-permute-start | bytes 786440 | tf_op jit(solution)/shard_map/while/body/eval_jaxpr/ppermute | solution.py:13
  148.5 12.6 %collective-permute-start.1 = (f32[4,128,128]{2,1,0:T(8,128)S(1)}, f32[4,128,128]{2,1,0:T(8,128)S(1)}, u32[]{:S(2)}, u32[]{:S(2)}) collective-permute-start(f32[4,128,128]{2,1,0:T(8,128)S(1)} %copy.54), channel_id=1, source_target_pairs={{16,0},{32,16},{48,32},{64,48},{80,64},{96,80},{112,96},{128,112},... | collective-permute-start | bytes 786440 | tf_op jit(solution)/shard_map/while/body/eval_jaxpr/ppermute | solution.py:13
  161.3 13.7 %collective-permute-start.1 = (f32[4,128,128]{2,1,0:T(8,128)S(1)}, f32[4,128,128]{2,1,0:T(8,128)S(1)}, u32[]{:S(2)}, u32[]{:S(2)}) collective-permute-start(f32[4,128,128]{2,1,0:T(8,128)S(1)} %copy.54), channel_id=1, source_target_pairs={{16,0},{32,16},{48,32},{64,48},{80,64},{96,80},{112,96},{128,112},... | collective-permute-start | bytes 786440 | tf_op jit(solution)/shard_map/while/body/eval_jaxpr/ppermute | solution.py:13
  175.1 12.8 %collective-permute-start.1 = (f32[4,128,128]{2,1,0:T(8,128)S(1)}, f32[4,128,128]{2,1,0:T(8,128)S(1)}, u32[]{:S(2)}, u32[]{:S(2)}) collective-permute-start(f32[4,128,128]{2,1,0:T(8,128)S(1)} %copy.54), channel_id=1, source_target_pairs={{16,0},{32,16},{48,32},{64,48},{80,64},{96,80},{112,96},{128,112},... | collective-permute-start | bytes 786440 | tf_op jit(solution)/shard_map/while/body/eval_jaxpr/ppermute | solution.py:13
  199.5 12.6 %collective-permute-start.1 = (f32[4,128,128]{2,1,0:T(8,128)S(1)}, f32[4,128,128]{2,1,0:T(8,128)S(1)}, u32[]{:S(2)}, u32[]{:S(2)}) collective-permute-start(f32[4,128,128]{2,1,0:T(8,128)S(1)} %copy.54), channel_id=1, source_target_pairs={{16,0},{32,16},{48,32},{64,48},{80,64},{96,80},{112,96},{128,112},... | collective-permute-start | bytes 786440 | tf_op jit(solution)/shard_map/while/body/eval_jaxpr/ppermute | solution.py:13
  212.2 13.7 %collective-permute-start.1 = (f32[4,128,128]{2,1,0:T(8,128)S(1)}, f32[4,128,128]{2,1,0:T(8,128)S(1)}, u32[]{:S(2)}, u32[]{:S(2)}) collective-permute-start(f32[4,128,128]{2,1,0:T(8,128)S(1)} %copy.54), channel_id=1, source_target_pairs={{16,0},{32,16},{48,32},{64,48},{80,64},{96,80},{112,96},{128,112},... | collective-permute-start | bytes 786440 | tf_op jit(solution)/shard_map/while/body/eval_jaxpr/ppermute | solution.py:13
  226.0 12.8 %collective-permute-start.1 = (f32[4,128,128]{2,1,0:T(8,128)S(1)}, f32[4,128,128]{2,1,0:T(8,128)S(1)}, u32[]{:S(2)}, u32[]{:S(2)}) collective-permute-start(f32[4,128,128]{2,1,0:T(8,128)S(1)} %copy.54), channel_id=1, source_target_pairs={{16,0},{32,16},{48,32},{64,48},{80,64},{96,80},{112,96},{128,112},... | collective-permute-start | bytes 786440 | tf_op jit(solution)/shard_map/while/body/eval_jaxpr/ppermute | solution.py:13
  250.4 12.6 %collective-permute-start.1 = (f32[4,128,128]{2,1,0:T(8,128)S(1)}, f32[4,128,128]{2,1,0:T(8,128)S(1)}, u32[]{:S(2)}, u32[]{:S(2)}) collective-permute-start(f32[4,128,128]{2,1,0:T(8,128)S(1)} %copy.54), channel_id=1, source_target_pairs={{16,0},{32,16},{48,32},{64,48},{80,64},{96,80},{112,96},{128,112},... | collective-permute-start | bytes 786440 | tf_op jit(solution)/shard_map/while/body/eval_jaxpr/ppermute | solution.py:13
  263.1 13.7 %collective-permute-start.1 = (f32[4,128,128]{2,1,0:T(8,128)S(1)}, f32[4,128,128]{2,1,0:T(8,128)S(1)}, u32[]{:S(2)}, u32[]{:S(2)}) collective-permute-start(f32[4,128,128]{2,1,0:T(8,128)S(1)} %copy.54), channel_id=1, source_target_pairs={{16,0},{32,16},{48,32},{64,48},{80,64},{96,80},{112,96},{128,112},... | collective-permute-start | bytes 786440 | tf_op jit(solution)/shard_map/while/body/eval_jaxpr/ppermute | solution.py:13
  277.0 12.8 %collective-permute-start.1 = (f32[4,128,128]{2,1,0:T(8,128)S(1)}, f32[4,128,128]{2,1,0:T(8,128)S(1)}, u32[]{:S(2)}, u32[]{:S(2)}) collective-permute-start(f32[4,128,128]{2,1,0:T(8,128)S(1)} %copy.54), channel_id=1, source_target_pairs={{16,0},{32,16},{48,32},{64,48},{80,64},{96,80},{112,96},{128,112},... | collective-permute-start | bytes 786440 | tf_op jit(solution)/shard_map/while/body/eval_jaxpr/ppermute | solution.py:13
  335.0 13.4 %collective-permute-start.3 = (f32[4,128,128]{2,1,0:T(8,128)S(1)}, f32[4,128,128]{2,1,0:T(8,128)S(1)}, u32[]{:S(2)}, u32[]{:S(2)}) collective-permute-start(f32[4,128,128]{2,1,0:T(8,128)S(1)} %copy.66), channel_id=1, source_target_pairs={{16,0},{32,16},{48,32},{64,48},{80,64},{96,80},{112,96},{128,112},... | collective-permute-start | bytes 786440 | tf_op jit(solution)/shard_map/while/body/eval_jaxpr/ppermute | solution.py:13
  348.5 13.1 %collective-permute-start.3 = (f32[4,128,128]{2,1,0:T(8,128)S(1)}, f32[4,128,128]{2,1,0:T(8,128)S(1)}, u32[]{:S(2)}, u32[]{:S(2)}) collective-permute-start(f32[4,128,128]{2,1,0:T(8,128)S(1)} %copy.66), channel_id=1, source_target_pairs={{16,0},{32,16},{48,32},{64,48},{80,64},{96,80},{112,96},{128,112},... | collective-permute-start | bytes 786440 | tf_op jit(solution)/shard_map/while/body/eval_jaxpr/ppermute | solution.py:13
  361.8 12.1 %collective-permute-start.3 = (f32[4,128,128]{2,1,0:T(8,128)S(1)}, f32[4,128,128]{2,1,0:T(8,128)S(1)}, u32[]{:S(2)}, u32[]{:S(2)}) collective-permute-start(f32[4,128,128]{2,1,0:T(8,128)S(1)} %copy.66), channel_id=1, source_target_pairs={{16,0},{32,16},{48,32},{64,48},{80,64},{96,80},{112,96},{128,112},... | collective-permute-start | bytes 786440 | tf_op jit(solution)/shard_map/while/body/eval_jaxpr/ppermute | solution.py:13
  374.1 13.0 %collective-permute-start.3 = (f32[4,128,128]{2,1,0:T(8,128)S(1)}, f32[4,128,128]{2,1,0:T(8,128)S(1)}, u32[]{:S(2)}, u32[]{:S(2)}) collective-permute-start(f32[4,128,128]{2,1,0:T(8,128)S(1)} %copy.66), channel_id=1, source_target_pairs={{16,0},{32,16},{48,32},{64,48},{80,64},{96,80},{112,96},{128,112},... | collective-permute-start | bytes 786440 | tf_op jit(solution)/shard_map/while/body/eval_jaxpr/ppermute | solution.py:13
  387.2 13.5 %collective-permute-start.3 = (f32[4,128,128]{2,1,0:T(8,128)S(1)}, f32[4,128,128]{2,1,0:T(8,128)S(1)}, u32[]{:S(2)}, u32[]{:S(2)}) collective-permute-start(f32[4,128,128]{2,1,0:T(8,128)S(1)} %copy.66), channel_id=1, source_target_pairs={{16,0},{32,16},{48,32},{64,48},{80,64},{96,80},{112,96},{128,112},... | collective-permute-start | bytes 786440 | tf_op jit(solution)/shard_map/while/body/eval_jaxpr/ppermute | solution.py:13
  425.0 13.0 %collective-permute-start.3 = (f32[4,128,128]{2,1,0:T(8,128)S(1)}, f32[4,128,128]{2,1,0:T(8,128)S(1)}, u32[]{:S(2)}, u32[]{:S(2)}) collective-permute-start(f32[4,128,128]{2,1,0:T(8,128)S(1)} %copy.66), channel_id=1, source_target_pairs={{16,0},{32,16},{48,32},{64,48},{80,64},{96,80},{112,96},{128,112},... | collective-permute-start | bytes 786440 | tf_op jit(solution)/shard_map/while/body/eval_jaxpr/ppermute | solution.py:13
  438.2 13.5 %collective-permute-start.3 = (f32[4,128,128]{2,1,0:T(8,128)S(1)}, f32[4,128,128]{2,1,0:T(8,128)S(1)}, u32[]{:S(2)}, u32[]{:S(2)}) collective-permute-start(f32[4,128,128]{2,1,0:T(8,128)S(1)} %copy.66), channel_id=1, source_target_pairs={{16,0},{32,16},{48,32},{64,48},{80,64},{96,80},{112,96},{128,112},... | collective-permute-start | bytes 786440 | tf_op jit(solution)/shard_map/while/body/eval_jaxpr/ppermute | solution.py:13
  476.0 13.0 %collective-permute-start.3 = (f32[4,128,128]{2,1,0:T(8,128)S(1)}, f32[4,128,128]{2,1,0:T(8,128)S(1)}, u32[]{:S(2)}, u32[]{:S(2)}) collective-permute-start(f32[4,128,128]{2,1,0:T(8,128)S(1)} %copy.66), channel_id=1, source_target_pairs={{16,0},{32,16},{48,32},{64,48},{80,64},{96,80},{112,96},{128,112},... | collective-permute-start | bytes 786440 | tf_op jit(solution)/shard_map/while/body/eval_jaxpr/ppermute | solution.py:13
  489.1 13.5 %collective-permute-start.3 = (f32[4,128,128]{2,1,0:T(8,128)S(1)}, f32[4,128,128]{2,1,0:T(8,128)S(1)}, u32[]{:S(2)}, u32[]{:S(2)}) collective-permute-start(f32[4,128,128]{2,1,0:T(8,128)S(1)} %copy.66), channel_id=1, source_target_pairs={{16,0},{32,16},{48,32},{64,48},{80,64},{96,80},{112,96},{128,112},... | collective-permute-start | bytes 786440 | tf_op jit(solution)/shard_map/while/body/eval_jaxpr/ppermute | solution.py:13
  526.9 13.0 %collective-permute-start.3 = (f32[4,128,128]{2,1,0:T(8,128)S(1)}, f32[4,128,128]{2,1,0:T(8,128)S(1)}, u32[]{:S(2)}, u32[]{:S(2)}) collective-permute-start(f32[4,128,128]{2,1,0:T(8,128)S(1)} %copy.66), channel_id=1, source_target_pairs={{16,0},{32,16},{48,32},{64,48},{80,64},{96,80},{112,96},{128,112},... | collective-permute-start | bytes 786440 | tf_op jit(solution)/shard_map/while/body/eval_jaxpr/ppermute | solution.py:13
  (56 other events, 495.8 us)
where the time goes:
time: 541 us
  waiting for transfers between devices  214 us (40%)
  starting transfers between devices  181 us (33%)
  matrix products  89.2 us (16%)
  blocking collectives  40.2 us (7%)
  other arithmetic  9.19 us (2%)
    ppermute x76, waiting for transfers between devices, shifted(): return lax.ppermute(block, axis, route)  214 us
    ppermute x76, starting transfers between devices, shifted(): return lax.ppermute(block, axis, route)  181 us
    dot_general x32, matrix products, accumulate(): return total + jnp.einsum('tab,axby->txy', weight, pairs, precision=highest)  57 us
    dot_general x32, matrix products, accumulate(): jnp.einsum('axk,bky->axby', left_blocks, right_blocks, precision=highest)  31.1 us
    all_gather x1, blocking collectives, on_device(): lax.all_gather(band_blocks, 'col', axis=0, tiled=True)  21.4 us
    all_gather x1, blocking collectives, on_device(): lax.all_gather(band_vectors, 'col', axis=0, tiled=True)  18.7 us
  transfers between devices with their start and end apart: 76, of which 42 were waited for; matrix products, arithmetic and copies ran while one was open for 18% of the time, Pallas kernels for 0%

commit v1 on v0

--- a/solution.py
+++ b/solution.py
@@ -94,6 +94,16 @@
 
 
 def on_device(core_blocks, block_coords, band_vectors, band_blocks, spread):
+
+    def review_indices(block_here):
+        part_next = jnp.concatenate(
+            lax.all_to_all(
+                jnp.stack(tuple((block_here for _ in range(lax.axis_size("col"))))), "col", 0, 0
+            ),
+            0,
+        )
+        return part_next
+
     row_count = lax.axis_size("row")
     column_count = lax.axis_size("col")
     tile_rows = NB // row_count
@@ -105,7 +115,7 @@
     layout = block_coords.reshape(row_count, slots, column_count, 2)
     targets = tile_layout(layout, this_row, this_col)
     vectors, blocks = (
-        lax.all_gather(band_vectors, "col", axis=0, tiled=True),
+        review_indices(band_vectors),
         lax.all_gather(band_blocks, "col", axis=0, tiled=True),
     )
     block_rows = this_row * tile_rows + targets[:, 0]

time: 541 us -> 525 us (0.970)
  blocking collectives: 40.2 us -> 18.4 us
  starting transfers between devices: 181 us -> 194 us
  waiting for transfers between devices: 214 us -> 207 us
    all_gather x1 -> x0, blocking collectives: 18.7 us -> none  [on_device(): lax.all_gather(band_vectors, 'col', axis=0, tiled=True)]
    ppermute x76, waiting for transfers between devices: 214 us -> 207 us  [shifted(): return lax.ppermute(block, axis, route)]
    all_to_all x0 -> x1, starting transfers between devices: none -> 7.42 us  [review_indices(): lax.all_to_all(jnp.stack(tuple((block_here for _ in range(lax.axis_size('...]
  transfers between devices with their start and end apart: 76 -> 77, of which waited for: 42 -> 45; matrix products, arithmetic and copies ran while one was open for 18% -> 19% of each run, Pallas kernels for 0% -> 0%
where the time goes in v1:
time: 525 us; the launch traced here: 524 us
  waiting for transfers between devices  207 us (39%)
  starting transfers between devices  194 us (37%)
  matrix products  89.2 us (17%)
  blocking collectives  18.4 us (4%)
  other arithmetic  9.19 us (2%)
    ppermute x76, waiting for transfers between devices, shifted(): return lax.ppermute(block, axis, route)  207 us
    ppermute x76, starting transfers between devices, shifted(): return lax.ppermute(block, axis, route)  186 us
    dot_general x32, matrix products, accumulate(): return total + jnp.einsum('tab,axby->txy', weight, pairs, precision=highest)  57 us
    dot_general x32, matrix products, accumulate(): jnp.einsum('axk,bky->axby', left_blocks, right_blocks, precision=highest)  31.1 us
    all_gather x1, blocking collectives, on_device(): lax.all_gather(band_blocks, 'col', axis=0, tiled=True)  18.4 us
  transfers between devices with their start and end apart: 77, of which 45 were waited for; matrix products, arithmetic and copies ran while one was open for 19% of the time, Pallas kernels for 0%

profile of v1, /device:TPU:6, one launch (start us, length us, event | category | flops | bytes accessed | tf_op | source)
XLA Modules:
  0.0 524.3 jit_solution(10217276417954414676)
XLA Ops:
  1.4 7.4 %all-to-all-start = ((f32[16,1,16,128]{3,2,1,0:T(8,128)}), f32[16,1,16,128]{3,2,1,0:T(8,128)S(1)}, u32[]{:S(2)}, u32[]{:S(2)}) async-start(f32[16,1,16,128]{3,2,1,0:T(8,128)} %stack.6), calls=%async_computation | async-start | bytes 262144 | tf_op jit(solution)/shard_map/all_to_all | solution.py:100
  10.3 18.4 %all-gather = s32[16,1,16]{2,1,0:T(1,128)S(1)} all-gather(s32[1,1,16]{2,1,0:T(1,128)S(1)} %bitcast.179), channel_id=1, replica_groups=mesh['row'=16,'col'=16] {'col'}, dimensions={0}, use_global_device_ids=true | all-gather | bytes 1088 | tf_op jit(solution)/shard_map/all_gather | solution.py:119
  30.5 6.0 %collective-permute-start.8 = (f32[4,128,128]{2,1,0:T(8,128)S(1)}, f32[4,128,128]{2,1,0:T(8,128)S(1)}, u32[]{:S(2)}, u32[]{:S(2)}) collective-permute-start(f32[4,128,128]{2,1,0:T(8,128)S(1)} %get-tuple-element.717), channel_id=1, source_target_pairs={{16,0},{32,16},{48,32},{64,48},{80,64},{96,80},{112,96},{128,112},... | collective-permute-start | bytes 786440 | tf_op jit(solution)/shard_map/ppermute | solution.py:13
  65.4 5.3 %collective-permute-done.6 = f32[1,4,128,128]{3,2,1,0:T(8,128)S(1)} collective-permute-done((f32[1,4,128,128]{3,2,1,0:T(8,128)S(1)}, f32[1,4,128,128]{3,2,1,0:T(8,128)S(1)}, u32[]{:S(2)}, u32[]{:S(2)}) %collective-permute-start.6) | collective-permute-done | bytes 262176 | tf_op jit(solution)/shard_map/ppermute | solution.py:13
  80.3 206.9 %while.42 = (s32[]{:T(128)}, f32[4,128,128]{2,0,1:T(4,128)S(1)}, f32[1,4,128,128]{3,2,1,0:T(8,128)S(1)}, f32[4,128,128]{2,1,0:T(8,128)S(1)}, s32[]{:T(128)}, /*i...) while((s32[]{:T(128)}, f32[4,128,128]{2,0,1:T(4,128)S(1)}, ...), condition=%wide.region_1.2_spmd.clone, body=%wide.region_0.1_spmd.clone.sunk | while | flops 415367424 | bytes 6292374 | solution.py:90
  80.5 6.5 %collective-permute-start.1 = (f32[4,128,128]{2,1,0:T(8,128)S(1)}, f32[4,128,128]{2,1,0:T(8,128)S(1)}, u32[]{:S(2)}, u32[]{:S(2)}) collective-permute-start(f32[4,128,128]{2,1,0:T(8,128)S(1)} %copy.62), channel_id=1, source_target_pairs={{16,0},{32,16},{48,32},{64,48},{80,64},{96,80},{112,96},{128,112},... | collective-permute-start | bytes 786440 | tf_op jit(solution)/shard_map/while/body/eval_jaxpr/ppermute | solution.py:13
  107.0 5.9 %collective-permute-start.1 = (f32[4,128,128]{2,1,0:T(8,128)S(1)}, f32[4,128,128]{2,1,0:T(8,128)S(1)}, u32[]{:S(2)}, u32[]{:S(2)}) collective-permute-start(f32[4,128,128]{2,1,0:T(8,128)S(1)} %copy.62), channel_id=1, source_target_pairs={{16,0},{32,16},{48,32},{64,48},{80,64},{96,80},{112,96},{128,112},... | collective-permute-start | bytes 786440 | tf_op jit(solution)/shard_map/while/body/eval_jaxpr/ppermute | solution.py:13
  115.9 5.9 %collective-permute-done.1 = f32[4,128,128]{2,1,0:T(8,128)S(1)} collective-permute-done((f32[4,128,128]{2,1,0:T(8,128)S(1)}, f32[4,128,128]{2,1,0:T(8,128)S(1)}, u32[]{:S(2)}, u32[]{:S(2)}) %collective-permute-start.1) | collective-permute-done | bytes 262176 | tf_op jit(solution)/shard_map/while/body/eval_jaxpr/ppermute | solution.py:13
  153.5 5.4 %collective-permute-done.1 = f32[4,128,128]{2,1,0:T(8,128)S(1)} collective-permute-done((f32[4,128,128]{2,1,0:T(8,128)S(1)}, f32[4,128,128]{2,1,0:T(8,128)S(1)}, u32[]{:S(2)}, u32[]{:S(2)}) %collective-permute-start.1) | collective-permute-done | bytes 262176 | tf_op jit(solution)/shard_map/while/body/eval_jaxpr/ppermute | solution.py:13
  166.9 5.9 %collective-permute-done.1 = f32[4,128,128]{2,1,0:T(8,128)S(1)} collective-permute-done((f32[4,128,128]{2,1,0:T(8,128)S(1)}, f32[4,128,128]{2,1,0:T(8,128)S(1)}, u32[]{:S(2)}, u32[]{:S(2)}) %collective-permute-start.1) | collective-permute-done | bytes 262176 | tf_op jit(solution)/shard_map/while/body/eval_jaxpr/ppermute | solution.py:13
  217.8 5.9 %collective-permute-done.1 = f32[4,128,128]{2,1,0:T(8,128)S(1)} collective-permute-done((f32[4,128,128]{2,1,0:T(8,128)S(1)}, f32[4,128,128]{2,1,0:T(8,128)S(1)}, u32[]{:S(2)}, u32[]{:S(2)}) %collective-permute-start.1) | collective-permute-done | bytes 262176 | tf_op jit(solution)/shard_map/while/body/eval_jaxpr/ppermute | solution.py:13
  268.7 5.9 %collective-permute-done.1 = f32[4,128,128]{2,1,0:T(8,128)S(1)} collective-permute-done((f32[4,128,128]{2,1,0:T(8,128)S(1)}, f32[4,128,128]{2,1,0:T(8,128)S(1)}, u32[]{:S(2)}, u32[]{:S(2)}) %collective-permute-start.1) | collective-permute-done | bytes 262176 | tf_op jit(solution)/shard_map/while/body/eval_jaxpr/ppermute | solution.py:13
  291.6 10.0 %collective-permute-done.13 = f32[1,4,128,128]{3,2,1,0:T(8,128)S(1)} collective-permute-done((f32[1,4,128,128]{3,2,1,0:T(8,128)S(1)}, f32[1,4,128,128]{3,2,1,0:T(8,128)S(1)}, u32[]{:S(2)}, u32[]{:S(2)}) %collective-permute-start.13) | collective-permute-done | bytes 262176 | tf_op jit(solution)/shard_map/ppermute | solution.py:13
  301.6 10.3 %collective-permute-done.14 = f32[1,4,128,128]{3,2,1,0:T(8,128)S(1)} collective-permute-done((f32[1,4,128,128]{3,2,1,0:T(8,128)S(1)}, f32[1,4,128,128]{3,2,1,0:T(8,128)S(1)}, u32[]{:S(2)}, u32[]{:S(2)}) %collective-permute-start.14) | collective-permute-done | bytes 262176 | tf_op jit(solution)/shard_map/ppermute | solution.py:13
  312.8 8.0 %collective-permute-done.15 = f32[1,4,128,128]{3,2,1,0:T(8,128)S(1)} collective-permute-done((f32[1,4,128,128]{3,2,1,0:T(8,128)S(1)}, f32[1,4,128,128]{3,2,1,0:T(8,128)S(1)}, u32[]{:S(2)}, u32[]{:S(2)}) %collective-permute-start.15) | collective-permute-done | bytes 262176 | tf_op jit(solution)/shard_map/ppermute | solution.py:13
  320.9 202.7 %while.43 = (s32[]{:T(128)}, f32[4,128,128]{2,0,1:T(4,128)S(1)}, f32[1,4,128,128]{3,2,1,0:T(8,128)S(1)}, f32[4,128,128]{2,1,0:T(8,128)S(1)}, s32[]{:T(128)}, /*i...) while((s32[]{:T(128)}, f32[4,128,128]{2,0,1:T(4,128)S(1)}, ...), condition=%wide.region_3.4_spmd.clone, body=%wide.region_2.3_spmd.clone.sunk | while | flops 415367424 | bytes 6292374 | solution.py:90
  355.3 6.3 %collective-permute-start.3 = (f32[4,128,128]{2,1,0:T(8,128)S(1)}, f32[4,128,128]{2,1,0:T(8,128)S(1)}, u32[]{:S(2)}, u32[]{:S(2)}) collective-permute-start(f32[4,128,128]{2,1,0:T(8,128)S(1)} %copy.74), channel_id=1, source_target_pairs={{16,0},{32,16},{48,32},{64,48},{80,64},{96,80},{112,96},{128,112},... | collective-permute-start | bytes 786440 | tf_op jit(solution)/shard_map/while/body/eval_jaxpr/ppermute | solution.py:13
  369.7 6.0 %collective-permute-start.3 = (f32[4,128,128]{2,1,0:T(8,128)S(1)}, f32[4,128,128]{2,1,0:T(8,128)S(1)}, u32[]{:S(2)}, u32[]{:S(2)}) collective-permute-start(f32[4,128,128]{2,1,0:T(8,128)S(1)} %copy.74), channel_id=1, source_target_pairs={{16,0},{32,16},{48,32},{64,48},{80,64},{96,80},{112,96},{128,112},... | collective-permute-start | bytes 786440 | tf_op jit(solution)/shard_map/while/body/eval_jaxpr/ppermute | solution.py:13
  378.8 5.6 %collective-permute-done.3 = f32[4,128,128]{2,1,0:T(8,128)S(1)} collective-permute-done((f32[4,128,128]{2,1,0:T(8,128)S(1)}, f32[4,128,128]{2,1,0:T(8,128)S(1)}, u32[]{:S(2)}, u32[]{:S(2)}) %collective-permute-start.3) | collective-permute-done | bytes 262176 | tf_op jit(solution)/shard_map/while/body/eval_jaxpr/ppermute | solution.py:13
  392.6 5.3 %collective-permute-done.3 = f32[4,128,128]{2,1,0:T(8,128)S(1)} collective-permute-done((f32[4,128,128]{2,1,0:T(8,128)S(1)}, f32[4,128,128]{2,1,0:T(8,128)S(1)}, u32[]{:S(2)}, u32[]{:S(2)}) %collective-permute-start.3) | collective-permute-done | bytes 262176 | tf_op jit(solution)/shard_map/while/body/eval_jaxpr/ppermute | solution.py:13
  428.7 5.5 %collective-permute-done.3 = f32[4,128,128]{2,1,0:T(8,128)S(1)} collective-permute-done((f32[4,128,128]{2,1,0:T(8,128)S(1)}, f32[4,128,128]{2,1,0:T(8,128)S(1)}, u32[]{:S(2)}, u32[]{:S(2)}) %collective-permute-start.3) | collective-permute-done | bytes 262176 | tf_op jit(solution)/shard_map/while/body/eval_jaxpr/ppermute | solution.py:13
  434.3 5.2 collective-permute-start.3
  442.5 5.9 %collective-permute-done.3 = f32[4,128,128]{2,1,0:T(8,128)S(1)} collective-permute-done((f32[4,128,128]{2,1,0:T(8,128)S(1)}, f32[4,128,128]{2,1,0:T(8,128)S(1)}, u32[]{:S(2)}, u32[]{:S(2)}) %collective-permute-start.3) | collective-permute-done | bytes 262176 | tf_op jit(solution)/shard_map/while/body/eval_jaxpr/ppermute | solution.py:13
  493.4 5.9 %collective-permute-done.3 = f32[4,128,128]{2,1,0:T(8,128)S(1)} collective-permute-done((f32[4,128,128]{2,1,0:T(8,128)S(1)}, f32[4,128,128]{2,1,0:T(8,128)S(1)}, u32[]{:S(2)}, u32[]{:S(2)}) %collective-permute-start.3) | collective-permute-done | bytes 262176 | tf_op jit(solution)/shard_map/while/body/eval_jaxpr/ppermute | solution.py:13
  (547 shorter events, 368.9 us)
Async XLA Ops:
  1.4 28.0 %all-to-all-start = ((f32[16,1,16,128]{3,2,1,0:T(8,128)}), f32[16,1,16,128]{3,2,1,0:T(8,128)S(1)}, u32[]{:S(2)}, u32[]{:S(2)}) async-start(f32[16,1,16,128]{3,2,1,0:T(8,128)} %stack.6), calls=%async_computation | async-start | bytes 262144 | tf_op jit(solution)/shard_map/all_to_all | solution.py:100
  45.1 12.6 %collective-permute-start.5 = (f32[1,4,128,128]{3,2,1,0:T(8,128)S(1)}, f32[1,4,128,128]{3,2,1,0:T(8,128)S(1)}, u32[]{:S(2)}, u32[]{:S(2)}) collective-permute-start(f32[1,4,128,128]{3,2,1,0:T(8,128)S(1)} %broadcast_select_fusion.5), channel_id=1, source_target_pairs={{2,0},{3,1},{4,2},{5,3},{6,4},{7,5},{8,6},{9,7},{10,8},{11,9},{12,... | collective-permute-start | bytes 786440 | tf_op jit(solution)/shard_map/ppermute | solution.py:13
  57.7 12.9 %collective-permute-start.6 = (f32[1,4,128,128]{3,2,1,0:T(8,128)S(1)}, f32[1,4,128,128]{3,2,1,0:T(8,128)S(1)}, u32[]{:S(2)}, u32[]{:S(2)}) collective-permute-start(f32[1,4,128,128]{3,2,1,0:T(8,128)S(1)} %broadcast_select_fusion.7), channel_id=1, source_target_pairs={{4,0},{5,1},{6,2},{7,3},{8,4},{9,5},{10,6},{11,7},{12,8},{13,9},{1... | collective-permute-start | bytes 786440 | tf_op jit(solution)/shard_map/ppermute | solution.py:13
  61.0 16.6 %collective-permute-start.11 = (f32[4,128,128]{2,1,0:T(8,128)S(1)}, f32[4,128,128]{2,1,0:T(8,128)S(1)}, u32[]{:S(2)}, u32[]{:S(2)}) collective-permute-start(f32[4,128,128]{2,1,0:T(8,128)S(1)} %broadcast_select_fusion.2), channel_id=1, source_target_pairs={{128,0},{144,16},{160,32},{176,48},{192,64},{208,80},{224,96},{240... | collective-permute-start | bytes 786440 | tf_op jit(solution)/shard_map/ppermute | solution.py:13
  94.2 12.6 %collective-permute-start.1 = (f32[4,128,128]{2,1,0:T(8,128)S(1)}, f32[4,128,128]{2,1,0:T(8,128)S(1)}, u32[]{:S(2)}, u32[]{:S(2)}) collective-permute-start(f32[4,128,128]{2,1,0:T(8,128)S(1)} %copy.62), channel_id=1, source_target_pairs={{16,0},{32,16},{48,32},{64,48},{80,64},{96,80},{112,96},{128,112},... | collective-permute-start | bytes 786440 | tf_op jit(solution)/shard_map/while/body/eval_jaxpr/ppermute | solution.py:13
  107.0 14.9 %collective-permute-start.1 = (f32[4,128,128]{2,1,0:T(8,128)S(1)}, f32[4,128,128]{2,1,0:T(8,128)S(1)}, u32[]{:S(2)}, u32[]{:S(2)}) collective-permute-start(f32[4,128,128]{2,1,0:T(8,128)S(1)} %copy.62), channel_id=1, source_target_pairs={{16,0},{32,16},{48,32},{64,48},{80,64},{96,80},{112,96},{128,112},... | collective-permute-start | bytes 786440 | tf_op jit(solution)/shard_map/while/body/eval_jaxpr/ppermute | solution.py:13
  145.7 13.2 %collective-permute-start.1 = (f32[4,128,128]{2,1,0:T(8,128)S(1)}, f32[4,128,128]{2,1,0:T(8,128)S(1)}, u32[]{:S(2)}, u32[]{:S(2)}) collective-permute-start(f32[4,128,128]{2,1,0:T(8,128)S(1)} %copy.62), channel_id=1, source_target_pairs={{16,0},{32,16},{48,32},{64,48},{80,64},{96,80},{112,96},{128,112},... | collective-permute-start | bytes 786440 | tf_op jit(solution)/shard_map/while/body/eval_jaxpr/ppermute | solution.py:13
  159.1 13.7 %collective-permute-start.1 = (f32[4,128,128]{2,1,0:T(8,128)S(1)}, f32[4,128,128]{2,1,0:T(8,128)S(1)}, u32[]{:S(2)}, u32[]{:S(2)}) collective-permute-start(f32[4,128,128]{2,1,0:T(8,128)S(1)} %copy.62), channel_id=1, source_target_pairs={{16,0},{32,16},{48,32},{64,48},{80,64},{96,80},{112,96},{128,112},... | collective-permute-start | bytes 786440 | tf_op jit(solution)/shard_map/while/body/eval_jaxpr/ppermute | solution.py:13
  172.9 12.5 %collective-permute-start.1 = (f32[4,128,128]{2,1,0:T(8,128)S(1)}, f32[4,128,128]{2,1,0:T(8,128)S(1)}, u32[]{:S(2)}, u32[]{:S(2)}) collective-permute-start(f32[4,128,128]{2,1,0:T(8,128)S(1)} %copy.62), channel_id=1, source_target_pairs={{16,0},{32,16},{48,32},{64,48},{80,64},{96,80},{112,96},{128,112},... | collective-permute-start | bytes 786440 | tf_op jit(solution)/shard_map/while/body/eval_jaxpr/ppermute | solution.py:13
  197.0 12.9 %collective-permute-start.1 = (f32[4,128,128]{2,1,0:T(8,128)S(1)}, f32[4,128,128]{2,1,0:T(8,128)S(1)}, u32[]{:S(2)}, u32[]{:S(2)}) collective-permute-start(f32[4,128,128]{2,1,0:T(8,128)S(1)} %copy.62), channel_id=1, source_target_pairs={{16,0},{32,16},{48,32},{64,48},{80,64},{96,80},{112,96},{128,112},... | collective-permute-start | bytes 786440 | tf_op jit(solution)/shard_map/while/body/eval_jaxpr/ppermute | solution.py:13
  210.0 13.7 %collective-permute-start.1 = (f32[4,128,128]{2,1,0:T(8,128)S(1)}, f32[4,128,128]{2,1,0:T(8,128)S(1)}, u32[]{:S(2)}, u32[]{:S(2)}) collective-permute-start(f32[4,128,128]{2,1,0:T(8,128)S(1)} %copy.62), channel_id=1, source_target_pairs={{16,0},{32,16},{48,32},{64,48},{80,64},{96,80},{112,96},{128,112},... | collective-permute-start | bytes 786440 | tf_op jit(solution)/shard_map/while/body/eval_jaxpr/ppermute | solution.py:13
  223.8 12.5 %collective-permute-start.1 = (f32[4,128,128]{2,1,0:T(8,128)S(1)}, f32[4,128,128]{2,1,0:T(8,128)S(1)}, u32[]{:S(2)}, u32[]{:S(2)}) collective-permute-start(f32[4,128,128]{2,1,0:T(8,128)S(1)} %copy.62), channel_id=1, source_target_pairs={{16,0},{32,16},{48,32},{64,48},{80,64},{96,80},{112,96},{128,112},... | collective-permute-start | bytes 786440 | tf_op jit(solution)/shard_map/while/body/eval_jaxpr/ppermute | solution.py:13
  247.9 12.9 %collective-permute-start.1 = (f32[4,128,128]{2,1,0:T(8,128)S(1)}, f32[4,128,128]{2,1,0:T(8,128)S(1)}, u32[]{:S(2)}, u32[]{:S(2)}) collective-permute-start(f32[4,128,128]{2,1,0:T(8,128)S(1)} %copy.62), channel_id=1, source_target_pairs={{16,0},{32,16},{48,32},{64,48},{80,64},{96,80},{112,96},{128,112},... | collective-permute-start | bytes 786440 | tf_op jit(solution)/shard_map/while/body/eval_jaxpr/ppermute | solution.py:13
  260.9 13.7 %collective-permute-start.1 = (f32[4,128,128]{2,1,0:T(8,128)S(1)}, f32[4,128,128]{2,1,0:T(8,128)S(1)}, u32[]{:S(2)}, u32[]{:S(2)}) collective-permute-start(f32[4,128,128]{2,1,0:T(8,128)S(1)} %copy.62), channel_id=1, source_target_pairs={{16,0},{32,16},{48,32},{64,48},{80,64},{96,80},{112,96},{128,112},... | collective-permute-start | bytes 786440 | tf_op jit(solution)/shard_map/while/body/eval_jaxpr/ppermute | solution.py:13
  274.8 12.5 %collective-permute-start.1 = (f32[4,128,128]{2,1,0:T(8,128)S(1)}, f32[4,128,128]{2,1,0:T(8,128)S(1)}, u32[]{:S(2)}, u32[]{:S(2)}) collective-permute-start(f32[4,128,128]{2,1,0:T(8,128)S(1)} %copy.62), channel_id=1, source_target_pairs={{16,0},{32,16},{48,32},{64,48},{80,64},{96,80},{112,96},{128,112},... | collective-permute-start | bytes 786440 | tf_op jit(solution)/shard_map/while/body/eval_jaxpr/ppermute | solution.py:13
  355.3 14.3 %collective-permute-start.3 = (f32[4,128,128]{2,1,0:T(8,128)S(1)}, f32[4,128,128]{2,1,0:T(8,128)S(1)}, u32[]{:S(2)}, u32[]{:S(2)}) collective-permute-start(f32[4,128,128]{2,1,0:T(8,128)S(1)} %copy.74), channel_id=1, source_target_pairs={{16,0},{32,16},{48,32},{64,48},{80,64},{96,80},{112,96},{128,112},... | collective-permute-start | bytes 786440 | tf_op jit(solution)/shard_map/while/body/eval_jaxpr/ppermute | solution.py:13
  369.7 14.7 %collective-permute-start.3 = (f32[4,128,128]{2,1,0:T(8,128)S(1)}, f32[4,128,128]{2,1,0:T(8,128)S(1)}, u32[]{:S(2)}, u32[]{:S(2)}) collective-permute-start(f32[4,128,128]{2,1,0:T(8,128)S(1)} %copy.74), channel_id=1, source_target_pairs={{16,0},{32,16},{48,32},{64,48},{80,64},{96,80},{112,96},{128,112},... | collective-permute-start | bytes 786440 | tf_op jit(solution)/shard_map/while/body/eval_jaxpr/ppermute | solution.py:13
  384.5 13.4 %collective-permute-start.3 = (f32[4,128,128]{2,1,0:T(8,128)S(1)}, f32[4,128,128]{2,1,0:T(8,128)S(1)}, u32[]{:S(2)}, u32[]{:S(2)}) collective-permute-start(f32[4,128,128]{2,1,0:T(8,128)S(1)} %copy.74), channel_id=1, source_target_pairs={{16,0},{32,16},{48,32},{64,48},{80,64},{96,80},{112,96},{128,112},... | collective-permute-start | bytes 786440 | tf_op jit(solution)/shard_map/while/body/eval_jaxpr/ppermute | solution.py:13
  420.9 13.2 %collective-permute-start.3 = (f32[4,128,128]{2,1,0:T(8,128)S(1)}, f32[4,128,128]{2,1,0:T(8,128)S(1)}, u32[]{:S(2)}, u32[]{:S(2)}) collective-permute-start(f32[4,128,128]{2,1,0:T(8,128)S(1)} %copy.74), channel_id=1, source_target_pairs={{16,0},{32,16},{48,32},{64,48},{80,64},{96,80},{112,96},{128,112},... | collective-permute-start | bytes 786440 | tf_op jit(solution)/shard_map/while/body/eval_jaxpr/ppermute | solution.py:13
  434.3 14.1 %collective-permute-start.3 = (f32[4,128,128]{2,1,0:T(8,128)S(1)}, f32[4,128,128]{2,1,0:T(8,128)S(1)}, u32[]{:S(2)}, u32[]{:S(2)}) collective-permute-start(f32[4,128,128]{2,1,0:T(8,128)S(1)} %copy.74), channel_id=1, source_target_pairs={{16,0},{32,16},{48,32},{64,48},{80,64},{96,80},{112,96},{128,112},... | collective-permute-start | bytes 786440 | tf_op jit(solution)/shard_map/while/body/eval_jaxpr/ppermute | solution.py:13
  448.5 12.7 %collective-permute-start.3 = (f32[4,128,128]{2,1,0:T(8,128)S(1)}, f32[4,128,128]{2,1,0:T(8,128)S(1)}, u32[]{:S(2)}, u32[]{:S(2)}) collective-permute-start(f32[4,128,128]{2,1,0:T(8,128)S(1)} %copy.74), channel_id=1, source_target_pairs={{16,0},{32,16},{48,32},{64,48},{80,64},{96,80},{112,96},{128,112},... | collective-permute-start | bytes 786440 | tf_op jit(solution)/shard_map/while/body/eval_jaxpr/ppermute | solution.py:13
  472.6 12.8 %collective-permute-start.3 = (f32[4,128,128]{2,1,0:T(8,128)S(1)}, f32[4,128,128]{2,1,0:T(8,128)S(1)}, u32[]{:S(2)}, u32[]{:S(2)}) collective-permute-start(f32[4,128,128]{2,1,0:T(8,128)S(1)} %copy.74), channel_id=1, source_target_pairs={{16,0},{32,16},{48,32},{64,48},{80,64},{96,80},{112,96},{128,112},... | collective-permute-start | bytes 786440 | tf_op jit(solution)/shard_map/while/body/eval_jaxpr/ppermute | solution.py:13
  485.6 13.7 %collective-permute-start.3 = (f32[4,128,128]{2,1,0:T(8,128)S(1)}, f32[4,128,128]{2,1,0:T(8,128)S(1)}, u32[]{:S(2)}, u32[]{:S(2)}) collective-permute-start(f32[4,128,128]{2,1,0:T(8,128)S(1)} %copy.74), channel_id=1, source_target_pairs={{16,0},{32,16},{48,32},{64,48},{80,64},{96,80},{112,96},{128,112},... | collective-permute-start | bytes 786440 | tf_op jit(solution)/shard_map/while/body/eval_jaxpr/ppermute | solution.py:13
  499.5 12.7 %collective-permute-start.3 = (f32[4,128,128]{2,1,0:T(8,128)S(1)}, f32[4,128,128]{2,1,0:T(8,128)S(1)}, u32[]{:S(2)}, u32[]{:S(2)}) collective-permute-start(f32[4,128,128]{2,1,0:T(8,128)S(1)} %copy.74), channel_id=1, source_target_pairs={{16,0},{32,16},{48,32},{64,48},{80,64},{96,80},{112,96},{128,112},... | collective-permute-start | bytes 786440 | tf_op jit(solution)/shard_map/while/body/eval_jaxpr/ppermute | solution.py:13
  (56 other events, 503.4 us)
